TPU v7x, 32 devices: a whole 2x2x4 slice. The times are simulated.
32 devices in a mesh: copy: 4 (over x, core), fsdp: 8 (over z, y).
Axes of the slice: x: 2, y: 2, z: 4, core: 2. Of those that a mesh axis runs over, the one named last changes fastest.
Arguments:
- student_hidden: bfloat16 [4, 32, 96, 1024], P('copy', 'fsdp'), may hold values from -6 to 6
- keep_index: int32 [4, 32, 96], P(None, 'fsdp'), may hold values from 0 to 191, as said below
- lengths: int32 [32], P('fsdp'), may hold values from 48 to 192
- teacher_layers: bfloat16 [4, 4, 8, 192, 1024], P(None, 'copy', 'fsdp')
- w_in: bfloat16 [1024, 2048], P('fsdp'), may hold values from -0.1875 to 0.1875
- w_out: bfloat16 [2048, 1024], P('fsdp'), may hold values from -0.125 to 0.125
- dec_in: bfloat16 [1024, 384], P('fsdp'), may hold values from -0.1875 to 0.1875
- dec_conv: bfloat16 [384, 2, 7, 384], P('fsdp'), may hold values from -0.125 to 0.125
- dec_out: bfloat16 [384, 1024], P('fsdp'), may hold values from -0.3125 to 0.3125
Outputs:
- loss: float32 [], replicated
- grad_hidden: bfloat16 [4, 32, 96, 1024], P('copy', 'fsdp')
- grad_w_in: bfloat16 [1024, 2048], P('fsdp')
- grad_w_out: bfloat16 [2048, 1024], P('fsdp')
- grad_dec_in: bfloat16 [1024, 384], P('fsdp')
- grad_dec_conv: bfloat16 [384, 2, 7, 384], P('fsdp')
- grad_dec_out: bfloat16 [384, 1024], P('fsdp')
Inputs may be any that keep to these rules, and one draw needn't show every extreme that they name: Each row keep_index[c, u, :] holds 96 distinct frame positions in rising order.
All inputs are finite; a program needn't handle non-finite values.
Results may differ from a plain program's by a relative error of at most 0.024.
Values may be sent and summed in bfloat16 or wider, within the bound.
A program may use at most 128 MiB of HBM per device.

v0:
```python
import math

import jax
import jax.numpy as jnp
from jax import lax
from jax.sharding import PartitionSpec as P

EPSILON = 1e-05
HALF_ROOT = 0.7071067811865476
GAUSS_PEAK = 0.3989422804014327


def layer_norm(values):
    center = values - jnp.mean(values, axis=-1, keepdims=True)
    inv_scale = lax.rsqrt(jnp.mean(center * center, axis=-1, keepdims=True) + EPSILON)
    return (center * inv_scale, inv_scale)


def norm_backward(grad, normed, inv_scale):
    return inv_scale * (
        grad
        - jnp.mean(grad, axis=-1, keepdims=True)
        - normed * jnp.mean(grad * normed, axis=-1, keepdims=True)
    )


def gelu_value(values):
    return 0.5 * values * (1.0 + lax.erf(values * HALF_ROOT))


def gelu_slope(values):
    return (
        0.5 * (1.0 + lax.erf(values * HALF_ROOT))
        + values * jnp.exp(-0.5 * values * values) * GAUSS_PEAK
    )


def unfold_frames(state, width):
    half = width // 2
    frames = state.shape[1]
    padded = jnp.pad(state, ((0, 0), (half, half), (0, 0)))
    return jnp.concatenate([padded[:, k : k + frames] for k in range(width)], axis=-1)


def fold_frames(grad, width, channels):
    units, frames = (grad.shape[0], grad.shape[1])
    half = width // 2
    split_grad = grad.reshape(units, frames, width, channels)
    padded = jnp.pad(split_grad, ((0, 0), (half, half), (0, 0), (0, 0)))
    total = jnp.zeros((units, frames, channels), grad.dtype)
    for k in range(width):
        total = total + padded[:, 2 * half - k : 2 * half - k + frames, k]
    return total


def kernel_matrix(kernels, layer):
    return jnp.transpose(kernels[:, layer], (1, 0, 2)).reshape(-1, kernels.shape[3])


def teacher_targets(layer_outputs, lengths):
    frames = layer_outputs.shape[2]
    valid = (jnp.arange(frames, dtype=jnp.int32)[None, :] < lengths[:, None]).astype(jnp.float32)
    weight = valid[:, :, None]
    count = jnp.sum(valid, axis=1)[:, None, None]
    total = jnp.zeros(layer_outputs.shape[1:], jnp.float32)
    for k in range(layer_outputs.shape[0]):
        values = layer_outputs[k].astype(jnp.float32)
        mean = jnp.sum(values * weight, axis=1, keepdims=True) / count
        center = values - mean
        variance = jnp.sum(center * center * weight, axis=1, keepdims=True) / count
        total = total + center * lax.rsqrt(variance + EPSILON)
    return (total * weight / layer_outputs.shape[0]).astype(jnp.bfloat16)


def contract_rows(left, right):
    return lax.dot_general(
        left, right, (((0,), (0,)), ((), ())), preferred_element_type=jnp.float32
    )


def contract_cols(left, right):
    return lax.dot_general(
        left, right, (((1,), (1,)), ((), ())), preferred_element_type=jnp.float32
    )


def on_device(
    student_hidden, keep_index, lengths, teacher_layers, w_in, w_out, dec_in, dec_conv, dec_out
):
    copy_index = lax.axis_index("copy")
    units, keep_count, width = (
        student_hidden.shape[1],
        student_hidden.shape[2],
        student_hidden.shape[3],
    )
    frames = teacher_layers.shape[3]
    per_copy = teacher_layers.shape[2]
    layers = dec_conv.shape[1]
    kernel = dec_conv.shape[2]
    channels = dec_conv.shape[3]
    rows = units * keep_count
    masked_count = frames - keep_count
    frame_index = jnp.arange(frames, dtype=jnp.int32)
    kept_all = jnp.any(keep_index[:, :, :, None] == frame_index[None, None, None, :], axis=2)
    valid = frame_index[None, :] < lengths[:, None]
    own_keep = lax.dynamic_index_in_dim(keep_index, copy_index, 0, keepdims=False)
    own_kept = lax.dynamic_index_in_dim(kept_all, copy_index, 0, keepdims=False)
    masked = jnp.logical_and(valid, jnp.logical_not(own_kept)).astype(jnp.float32)
    unit_index = jnp.arange(units, dtype=jnp.int32)[:, None]
    own_lengths = lax.dynamic_slice_in_dim(lengths, copy_index * per_copy, per_copy, 0)
    own_targets = teacher_targets(teacher_layers[:, 0], own_lengths)
    targets = lax.all_gather(own_targets, "copy", axis=0, tiled=True)
    hidden_rows = student_hidden[0].reshape(rows, width).astype(jnp.float32)
    normed_exact, inv_scale = layer_norm(hidden_rows)
    normed = normed_exact.astype(jnp.bfloat16)
    w_in_all, w_out_all, dec_in_all, dec_conv_all, dec_out_all = (
        lax.all_gather(w_in, "fsdp", axis=0, tiled=True),
        lax.all_gather(w_out, "fsdp", axis=0, tiled=True),
        lax.all_gather(dec_in, "fsdp", axis=0, tiled=True),
        lax.all_gather(dec_conv, "fsdp", axis=0, tiled=True),
        lax.all_gather(dec_out, "fsdp", axis=0, tiled=True),
    )
    projected = jnp.dot(normed, w_in_all, preferred_element_type=jnp.float32)
    activation = gelu_value(projected).astype(jnp.bfloat16)
    mixed = jnp.dot(activation, w_out_all, preferred_element_type=jnp.float32)
    student_out = (hidden_rows + mixed).astype(jnp.bfloat16)
    lifted = jnp.dot(student_out, dec_in_all, preferred_element_type=jnp.float32).astype(
        jnp.bfloat16
    )
    state = (
        jnp.zeros((units, frames, channels), jnp.bfloat16)
        .at[unit_index, own_keep]
        .set(lifted.reshape(units, keep_count, channels))
    )
    saved = []
    for layer in range(layers):
        unfolded = unfold_frames(state, kernel).reshape(units * frames, kernel * channels)
        convolved = jnp.dot(
            unfolded, kernel_matrix(dec_conv_all, layer), preferred_element_type=jnp.float32
        )
        conv_normed, conv_scale = layer_norm(convolved)
        result = gelu_value(conv_normed)
        if layer > 0:
            result = result + state.reshape(units * frames, channels).astype(jnp.float32)
        saved.append((unfolded, conv_normed, conv_scale))
        state = result.reshape(units, frames, channels).astype(jnp.bfloat16)
    final_state = state.reshape(units * frames, channels)
    prediction = jnp.dot(final_state, dec_out_all, preferred_element_type=jnp.float32)
    loss_scale = 1.0 / math.sqrt(width)
    error = (
        prediction - targets.reshape(units * frames, width).astype(jnp.float32)
    ) * masked.reshape(units * frames, 1)
    total = jnp.sum(error * error) * loss_scale
    prediction_grad = (2.0 * loss_scale * error).astype(jnp.bfloat16)
    out_term = contract_rows(final_state, prediction_grad)
    state_grad = contract_cols(prediction_grad, dec_out_all)
    kernel_terms = [None] * layers
    for layer in reversed(range(layers)):
        unfolded, conv_normed, conv_scale = saved[layer]
        filter_grad = norm_backward(
            state_grad * gelu_slope(conv_normed), conv_normed, conv_scale
        ).astype(jnp.bfloat16)
        kernel_terms[layer] = contract_rows(unfolded, filter_grad)
        unfold_grad = contract_cols(filter_grad, kernel_matrix(dec_conv_all, layer))
        previous_grad = fold_frames(
            unfold_grad.reshape(units, frames, kernel * channels), kernel, channels
        ).reshape(units * frames, channels)
        if layer > 0:
            previous_grad = previous_grad + state_grad
        state_grad = previous_grad
    conv_term = jnp.stack(
        [
            jnp.transpose(term.reshape(kernel, channels, channels), (1, 0, 2))
            for term in kernel_terms
        ],
        axis=1,
    )
    lifted_grad = (
        jnp.take_along_axis(
            state_grad.reshape(units, frames, channels), own_keep[:, :, None], axis=1
        )
        .reshape(rows, channels)
        .astype(jnp.bfloat16)
    )
    in_term = contract_rows(student_out, lifted_grad)
    output_grad = contract_cols(lifted_grad, dec_in_all)
    output_half = output_grad.astype(jnp.bfloat16)
    activation_grad = contract_cols(output_half, w_out_all)
    projected_grad = (activation_grad * gelu_slope(projected)).astype(jnp.bfloat16)
    normed_grad = contract_cols(projected_grad, w_in_all)
    grad_hidden = (output_grad + norm_backward(normed_grad, normed_exact, inv_scale)).astype(
        jnp.bfloat16
    )
    input_share = lax.psum_scatter(
        contract_rows(normed, projected_grad).astype(jnp.bfloat16),
        "fsdp",
        scatter_dimension=0,
        tiled=True,
    )
    output_share = lax.psum_scatter(
        contract_rows(activation, output_half).astype(jnp.bfloat16),
        "fsdp",
        scatter_dimension=0,
        tiled=True,
    )
    decoder_in_share, decoder_conv_share, decoder_out_share = (
        lax.psum_scatter(
            in_term.astype(jnp.bfloat16), "fsdp", scatter_dimension=0, tiled=True
        ).astype(jnp.float32),
        lax.psum_scatter(
            conv_term.astype(jnp.bfloat16), "fsdp", scatter_dimension=0, tiled=True
        ).astype(jnp.float32),
        lax.psum_scatter(
            out_term.astype(jnp.bfloat16), "fsdp", scatter_dimension=0, tiled=True
        ).astype(jnp.float32),
    )
    summed = (
        lax.psum(input_share, "copy").astype(jnp.float32),
        lax.psum(output_share, "copy").astype(jnp.float32),
        lax.psum(decoder_in_share.astype(jnp.bfloat16), "copy").astype(jnp.float32),
        lax.psum(decoder_conv_share.astype(jnp.bfloat16), "copy").astype(jnp.float32),
        lax.psum(decoder_out_share.astype(jnp.bfloat16), "copy").astype(jnp.float32),
    )
    loss_total = lax.psum(total, ("copy", "fsdp"))
    slot_total = lax.axis_size("copy") * lax.axis_size("fsdp") * units * masked_count
    loss = loss_total / float(slot_total)
    return (
        loss,
        grad_hidden.reshape(1, units, keep_count, width),
        summed[0].astype(jnp.bfloat16),
        summed[1].astype(jnp.bfloat16),
        summed[2].astype(jnp.bfloat16),
        summed[3].astype(jnp.bfloat16),
        summed[4].astype(jnp.bfloat16),
    )


def solution(mesh):
    placed = (
        P("copy", "fsdp", None, None),
        P(None, "fsdp", None),
        P("fsdp"),
        P(None, "copy", "fsdp", None, None),
        P("fsdp", None),
        P("fsdp", None),
        P("fsdp", None),
        P("fsdp", None, None, None),
        P("fsdp", None),
    )
    return jax.shard_map(
        on_device,
        mesh=mesh,
        in_specs=placed,
        out_specs=(
            P(),
            P("copy", "fsdp", None, None),
            P("fsdp", None),
            P("fsdp", None),
            P("fsdp", None),
            P("fsdp", None, None, None),
            P("fsdp", None),
        ),
        check_vma=False,
    )
```

profile of v0, /device:TPU:9, one launch (start us, length us, event | category | flops | bytes accessed | tf_op | source)
XLA Modules:
  0.0 766.8 jit_solution(7713880642674968786)
XLA Ops:
  7.2 2.0 copy.27
  11.4 1.2 fusion.81
  18.3 1.2 fusion.60
  21.2 27.7 %all_gather.20 = bf16[1024,384]{1,0:T(8,128)(2,1)S(1)} all-gather(bf16[128,384]{1,0:T(8,128)(2,1)S(1)} %copy-done.17), channel_id=1, replica_groups=mesh['copy'=4,'fsdp'=8] {'fsdp'}, dimensions={0}, use_global_device_ids=true | all-gather | bytes 884736 | tf_op jit(solution)/shard_map/all_gather | solution.py:119
  48.9 32.5 %all_gather.22 = bf16[384,1024]{1,0:T(8,128)(2,1)} all-gather(bf16[48,1024]{1,0:T(8,128)(2,1)S(1)} %copy-done.18), channel_id=1, replica_groups=mesh['copy'=4,'fsdp'=8] {'fsdp'}, dimensions={0}, use_global_device_ids=true | all-gather | bytes 884736 | tf_op jit(solution)/shard_map/all_gather | solution.py:121
  81.7 21.3 %all-gather.9.cloned.1.call-done = bf16[384,2,7,384]{3,0,2,1:T(8,128)(2,1)} async-done(((bf16[48,2,7,384]{3,0,2,1:T(8,128)(2,1)}), bf16[384,2,7,384]{3,0,2,1:T(8,128)(2,1)}) %all-gather.9.cloned.1.call-update) | async-done | bytes 4128784 | tf_op jit(solution)/shard_map/all_gather | solution.py:120
  103.0 4.6 fusion.90
  107.6 68.5 %all-gather.5.cloned.1.call-done = bf16[1024,2048]{1,0:T(8,128)(2,1)} async-done(((bf16[128,2048]{1,0:T(8,128)(2,1)}), bf16[1024,2048]{1,0:T(8,128)(2,1)}) %all-gather.5.cloned.1.call-update) | async-done | bytes 4194320 | tf_op jit(solution)/shard_map/all_gather | solution.py:117
  176.1 5.7 multiply_convert_fusion.1
  181.8 67.8 %all-gather.7.cloned.1.call-done = bf16[2048,1024]{1,0:T(8,128)(2,1)} async-done(((bf16[256,1024]{1,0:T(8,128)(2,1)}), bf16[2048,1024]{1,0:T(8,128)(2,1)}) %all-gather.7.cloned.1.call-update) | async-done | bytes 4194320 | tf_op jit(solution)/shard_map/all_gather | solution.py:118
  249.6 4.5 fusion.22
  254.7 22.3 %scatter_fusion = bf16[4,192,384]{2,1,0:T(8,128)(2,1)S(1)} fusion(bf16[4,192,384]{2,1,0:T(8,128)(2,1)S(1)} %broadcast_in_dim.12, s32[384]{0:T(512)S(1)} %reshape.991, bf16[384,384]{1,0:T(8,128)(2,1)S(1)} %convolution_convert_fusion.4), kind=kCustom, calls=%fused_computation.1 | custom fusion | bytes 887808 | tf_op jit(solution)/shard_map/scatter | solution.py:133
  278.3 1.0 copy-done.11
  279.3 2.4 fusion.91
  283.7 1.0 copy-done.10
  284.7 2.4 fusion.92
  287.5 1.9 add_convert_fusion
  289.5 3.8 multiply_convert_fusion
  293.3 1.2 copy-done.24
  294.5 1.7 convolution_convert_fusion.2
  296.2 4.2 fusion.87
  300.5 1.8 multiply_convert_fusion.3
  302.3 0.8 copy-done.8
  303.1 4.0 fusion.9
  308.3 1.3 fusion.86
  310.5 2.4 fusion.7
  313.6 3.7 gather_fusion
  317.3 2.8 convolution_convert_fusion.3
  320.2 6.5 copy.29
  326.7 6.6 copy.28
  333.3 4.6 convert_bitcast_fusion
  337.9 2.4 convert_bitcast_fusion.1
  340.3 2.4 pad_maximum_fusion
  343.0 0.9 copy-done.7
  345.3 4.4 convolution_convert_fusion
  349.7 6.3 fusion.5
  356.0 1.1 copy-done.26
  357.2 4.4 convolution_convert_fusion.1
  362.3 65.2 %reduce-scatter.10.cloned.1.call-done = bf16[128,384]{1,0:T(8,128)(2,1)} async-done(((bf16[1024,384]{1,0:T(8,128)(2,1)}), bf16[128,384]{1,0:T(8,128)(2,1)}) %reduce-scatter.10.cloned.1.call-update) | async-done | bytes 98320 | tf_op jit(solution)/shard_map/reduce_scatter | solution.py:207
  427.5 91.5 %reduce-scatter.12.cloned.1.call-done = bf16[48,2,7,384]{3,0,2,1:T(8,128)(2,1)} async-done(((bf16[384,2,7,384]{3,0,2,1:T(8,128)(2,1)}), bf16[48,2,7,384]{3,0,2,1:T(8,128)(2,1)}) %reduce-scatter.12.cloned.1.call-update) | async-done | bytes 516112 | tf_op jit(solution)/shard_map/reduce_scatter | solution.py:210
  519.0 91.8 %reduce-scatter.8.cloned.1.call-done = bf16[256,1024]{1,0:T(8,128)(2,1)} async-done(((bf16[2048,1024]{1,0:T(8,128)(2,1)}), bf16[256,1024]{1,0:T(8,128)(2,1)}) %reduce-scatter.8.cloned.1.call-update) | async-done | bytes 524304 | tf_op jit(solution)/shard_map/reduce_scatter | solution.py:200
  610.8 91.6 %reduce-scatter.6.cloned.1.call-done = bf16[128,2048]{1,0:T(8,128)(2,1)} async-done(((bf16[1024,2048]{1,0:T(8,128)(2,1)}), bf16[128,2048]{1,0:T(8,128)(2,1)}) %reduce-scatter.6.cloned.1.call-update) | async-done | bytes 524304 | tf_op jit(solution)/shard_map/reduce_scatter | solution.py:194
  702.4 5.7 fusion.85
  708.1 40.8 %psum.42 = f32[]{:T(128)} all-reduce(f32[]{:T(128)S(6)} %mul.474), channel_id=1, replica_groups=mesh['copy'=4,'fsdp'=8] {'copy','fsdp'}, use_global_device_ids=true, to_apply=%region_18.19 | all-reduce | flops 1 | bytes 8 | tf_op jit(solution)/shard_map/psum | solution.py:224
  749.6 2.8 fusion.21
  752.4 2.3 copy.30
  754.7 1.9 copy.51
  756.6 0.8 copy.52
  (136 shorter events, 19.7 us)
Async XLA Ops:
  7.2 3.6 copy-start.22
  7.2 6.1 copy-start.1
  7.2 95.8 %all-gather.9.cloned.1.call-start = ((), (), s32[]{:S(2)}) async-start(), calls=%async_computation.7 | async-start | bytes 4644864 | tf_op jit(solution)/shard_map/all_gather | solution.py:120
  9.3 166.8 %all-gather.5.cloned.1.call-start = ((), (), s32[]{:S(2)}) async-start(), calls=%async_computation.5 | async-start | bytes 4718592 | tf_op jit(solution)/shard_map/all_gather | solution.py:117
  10.0 239.6 %all-gather.7.cloned.1.call-start = ((), (), s32[]{:S(2)}) async-start(), calls=%async_computation.6 | async-start | bytes 4718592 | tf_op jit(solution)/shard_map/all_gather | solution.py:118
  10.7 278.7 %all-gather.11.cloned.1.call-start = ((), (), s32[]{:S(2)}) async-start(), calls=%async_computation.8 | async-start | bytes 1966080 | tf_op jit(solution)/shard_map/all_gather | solution.py:112
  16.5 3.1 copy-start.2
  18.3 2.0 copy-start.21
  18.3 2.9 copy-start.17
  19.5 29.4 %copy-start.18 = (bf16[48,1024]{1,0:T(8,128)(2,1)S(1)}, bf16[48,1024]{1,0:T(8,128)(2,1)}, u32[]{:S(2)}) copy-start(bf16[48,1024]{1,0:T(8,128)(2,1)} %param.17) | copy-start | bytes 294916
  19.6 342.7 %reduce-scatter.14.cloned.1.call-start = ((), (), s32[]{:S(2)}) async-start(), calls=%async_computation.13 | async-start | bytes 884736 | tf_op jit(solution)/shard_map/reduce_scatter | solution.py:213
  48.9 205.1 %copy-start.6 = (bf16[1024,384]{1,0:T(8,128)(2,1)}, bf16[1024,384]{1,0:T(8,128)(2,1)S(1)}, u32[]{:S(2)}) copy-start(bf16[1024,384]{1,0:T(8,128)(2,1)S(1)} %all_gather.20) | copy-start | bytes 2359300
  81.7 94.4 %copy-start.13 = (bf16[384,1024]{1,0:T(8,128)(2,1)}, bf16[384,1024]{1,0:T(8,128)(2,1)S(1)}, u32[]{:S(2)}) copy-start(bf16[384,1024]{1,0:T(8,128)(2,1)S(1)} %fusion.16) | copy-start | bytes 2359300
  254.1 23.0 %copy-start.23 = (bf16[384,1024]{1,0:T(8,128)(2,1)}, bf16[384,1024]{1,0:T(8,128)(2,1)S(1)}, u32[]{:S(2)}) copy-start(bf16[384,1024]{1,0:T(8,128)(2,1)S(1)} %fusion.22) | copy-start | bytes 2359300
  277.7 1.6 copy-start.11
  278.3 3.4 copy-start.3
  283.1 1.6 copy-start.10
  283.7 3.5 copy-start.4
  289.5 5.1 copy-start.15
  293.3 1.2 copy-start.24
  300.4 127.0 %reduce-scatter.10.cloned.1.call-start = ((), (), s32[]{:S(2)}) async-start(), calls=%async_computation.11 | async-start | bytes 884736 | tf_op jit(solution)/shard_map/reduce_scatter | solution.py:207
  302.3 0.8 copy-start.8
  307.0 1.3 copy-start.12
  308.3 2.2 copy-start
  320.2 198.8 %reduce-scatter.12.cloned.1.call-start = ((), (), s32[]{:S(2)}) async-start(), calls=%async_computation.12 | async-start | bytes 4644864 | tf_op jit(solution)/shard_map/reduce_scatter | solution.py:210
  326.7 6.6 copy-start.9
  333.3 4.7 copy-start.5
  342.7 1.1 copy-start.7
  342.8 268.1 %reduce-scatter.8.cloned.1.call-start = ((), (), s32[]{:S(2)}) async-start(), calls=%async_computation.10 | async-start | bytes 4718592 | tf_op jit(solution)/shard_map/reduce_scatter | solution.py:200
  343.9 1.4 copy-start.25
  349.7 352.7 %reduce-scatter.6.cloned.1.call-start = ((), (), s32[]{:S(2)}) async-start(), calls=%async_computation.9 | async-start | bytes 4718592 | tf_op jit(solution)/shard_map/reduce_scatter | solution.py:194
  349.7 7.4 copy-start.14
  356.0 1.1 copy-start.26
  361.6 390.8 %all-reduce.7.cloned.1.call-start = ((), (), s32[]{:S(2)}) async-start(), calls=%async_computation.14 | async-start | bytes 3522560 | tf_op jit(solution)/shard_map/psum | solution.py:218
  752.4 4.2 copy-start.16
  752.4 5.0 copy-start.20
  752.4 5.6 copy-start.19
Sparse Core Ops, SparseCore 0:
  10.8 92.1 all-gather.8
  105.1 70.9 all-gather.4
  178.2 71.3 all-gather.6
  251.6 20.5 all-gather.10
  300.6 61.4 reduce-scatter.13
  365.2 62.2 reduce-scatter.9
  431.1 87.8 reduce-scatter.11
  522.6 88.1 reduce-scatter.7
  614.5 87.8 reduce-scatter.5
  705.0 47.0 all-reduce.6
where the time goes:
time: 779 us; the launch traced here: 767 us
  waiting for transfers between devices  499 us (64%)
  blocking collectives  101 us (13%)
  local copies, waits for them, and re-layouts  63.5 us (8%)
  matrix products  62.8 us (8%)
  other arithmetic  22.4 us (3%)
  between operations  17.4 us (2%)
    reduce_scatter x1, waiting for transfers between devices, on_device(): lax.psum_scatter(contract_rows(activation, output_half).astype(jnp.bfloat...  91.8 us
    reduce_scatter x1, waiting for transfers between devices, on_device(): lax.psum_scatter(contract_rows(normed, projected_grad).astype(jnp.bfloat1...  91.6 us
    reduce_scatter x1, waiting for transfers between devices, on_device(): lax.psum_scatter(conv_term.astype(jnp.bfloat16), 'fsdp', scatter_dimensio...  91.5 us
    all_gather x1, waiting for transfers between devices, on_device(): lax.all_gather(w_in, 'fsdp', axis=0, tiled=True)  68.5 us
    all_gather x1, waiting for transfers between devices, on_device(): lax.all_gather(w_out, 'fsdp', axis=0, tiled=True)  67.8 us
    reduce_scatter x1, waiting for transfers between devices, on_device(): lax.psum_scatter(in_term.astype(jnp.bfloat16), 'fsdp', scatter_dimension=...  65.2 us
    psum x1, blocking collectives, on_device(): loss_total = lax.psum(total, ('copy', 'fsdp'))  40.8 us
    all_gather x1, blocking collectives, on_device(): lax.all_gather(dec_out, 'fsdp', axis=0, tiled=True)  32.5 us
  transfers between devices with their start and end apart: 10, of which 7 were waited for; matrix products, arithmetic and copies ran while one was open for 16% of the time, Pallas kernels for 0%

commit v1 on v0

--- a/solution.py
+++ b/solution.py
@@ -3,6 +3,8 @@
 import jax
 import jax.numpy as jnp
 from jax import lax
+from jax.experimental import pallas as pl
+from jax.experimental.pallas import tpu as pltpu
 from jax.sharding import PartitionSpec as P
 
 EPSILON = 1e-05
@@ -32,6 +34,413 @@
     return (
         0.5 * (1.0 + lax.erf(values * HALF_ROOT))
         + values * jnp.exp(-0.5 * values * values) * GAUSS_PEAK
+    )
+
+
+MESH = pl.DeviceIdType.MESH
+VMEM_LIMIT = 60 * 1024 * 1024
+
+
+class Place:
+    def __init__(self, groups):
+        copy, shard = lax.axis_index("copy"), lax.axis_index("fsdp")
+        self.groups = groups
+        self.copy, self.shard = copy, shard
+        self.x, self.h = copy // 2, copy % 2
+        self.a, self.b = shard // 2, shard % 2
+        self.core_peer = (self.x * 2 + 1 - self.h, shard)
+        self.x_peer = ((1 - self.x) * 2 + self.h, shard)
+        self.y_peer = (copy, self.a * 2 + 1 - self.b)
+
+    def later(self, d):
+        return lax.rem(self.a + d, self.groups)
+
+    def earlier(self, d):
+        return lax.rem(self.a + self.groups - d, self.groups)
+
+    def z_peer(self, d):
+        return (self.copy, self.later(d) * 2 + self.b)
+
+    def greet(self):
+        barrier = pltpu.get_barrier_semaphore()
+        peers = [self.core_peer, self.x_peer, self.y_peer]
+        peers += [self.z_peer(d) for d in range(1, self.groups)]
+        for peer in peers:
+            pl.semaphore_signal(barrier, inc=1, device_id=peer, device_id_type=MESH)
+        pl.semaphore_wait(barrier, len(peers))
+
+
+class Sender:
+    def __init__(self, send_sem, recv_sem):
+        self.send_sem, self.recv_sem, self.count, self.started = send_sem, recv_sem, 0, []
+
+    def send(self, src, dst, peer):
+        copy = pltpu.make_async_remote_copy(
+            src_ref=src,
+            dst_ref=dst,
+            send_sem=self.send_sem.at[self.count],
+            recv_sem=self.recv_sem.at[self.count],
+            device_id=peer,
+            device_id_type=MESH,
+        )
+        copy.start()
+        self.count += 1
+        self.started.append(copy)
+        return copy
+
+    def drain(self):
+        for copy in self.started:
+            copy.wait_send()
+
+
+def columns(index, size):
+    return pl.ds(pl.multiple_of(index * size, 128), size)
+
+
+def wavefront(stages, count):
+    for step in range(count + len(stages) - 1):
+        for number, stage in reversed(list(enumerate(stages))):
+            if 0 <= step - number < count:
+                stage(step - number)
+
+
+def gather_kernel(groups, quarter, w_in, w_out, conv, dec_out, dec_in, own_targets,
+                  w_in_all, w_out_all, conv_all, dec_out_all, dec_in_all, targets,
+                  send_sem, recv_sem, local_sem):
+    at = Place(groups)
+    a, b, h, x = at.a, at.b, at.h, at.x
+    half = 2 * quarter
+    sender = Sender(send_sem, recv_sem)
+    ins = (w_in, w_out, conv, dec_out, dec_in)
+    outs = (w_in_all, w_out_all, conv_all, dec_out_all, dec_in_all)
+    split = (True, True, False, True, False)
+    own = (
+        w_in.at[h, x], w_out.at[h, x], conv.at[h], dec_out.at[:, columns(2 * h + x, quarter)], dec_in.at[h],
+    )
+
+    def piece(t, i, j):
+        if t < 2:
+            return outs[t].at[i, j, h, x]
+        if t == 2:
+            return outs[t].at[h, :, i, j]
+        if t == 3:
+            return outs[t].at[i, j, :, columns(2 * h + x, quarter)]
+        return outs[t].at[i, j, h]
+
+    def both(t, i):
+        if t < 2:
+            return outs[t].at[i, :, h, x]
+        return outs[t].at[i, :, :, columns(2 * h + x, quarter)]
+
+    def half_piece(t, i, j):
+        if t == 3:
+            return outs[t].at[i, j, :, columns(h, half)]
+        if t < 2:
+            return outs[t].at[i, j, h]
+        return piece(t, i, j)
+
+    def half_both(t, i):
+        if t == 2:
+            return outs[t].at[h, :, i]
+        if t == 3:
+            return outs[t].at[i, :, :, columns(h, half)]
+        return outs[t].at[i, :, h]
+
+    at.greet()
+    locals_ = []
+    for t in range(5):
+        place = outs[t].at[:, :, a, b] if t == 2 else outs[t].at[a, b]
+        locals_.append(pltpu.make_async_copy(ins[t], place, local_sem.at[t]))
+    locals_.append(pltpu.make_async_copy(own_targets, targets.at[at.copy], local_sem.at[5]))
+    for copy in locals_:
+        copy.start()
+    z_copies, y_copies, x_copies, core_copies = {}, {}, {}, {}
+    for t in range(5):
+        for d in range(1, groups):
+            z_copies[t, d] = sender.send(own[t], piece(t, a, b), at.z_peer(d))
+        y_copies[t, 0] = sender.send(own[t], piece(t, a, b), at.y_peer)
+    target_x = sender.send(own_targets, targets.at[at.copy], at.x_peer)
+    target_core = sender.send(own_targets, targets.at[at.copy], at.core_peer)
+
+    def after_z(t):
+        for d in range(1, groups):
+            z_copies[t, d].wait_recv()
+            block = piece(t, at.earlier(d), b)
+            y_copies[t, d] = sender.send(block, block, at.y_peer)
+
+    def after_y(t):
+        for d in range(groups):
+            y_copies[t, d].wait_recv()
+            i = at.earlier(d)
+            if split[t]:
+                block = both(t, i) if d else piece(t, i, 1 - b)
+                x_copies[t, d] = sender.send(block, block, at.x_peer)
+            else:
+                block = half_both(t, i) if d else half_piece(t, i, 1 - b)
+                core_copies[t, d] = sender.send(block, block, at.core_peer)
+
+    def after_x(t):
+        if split[t]:
+            for d in range(groups):
+                x_copies[t, d].wait_recv()
+                i = at.earlier(d)
+                block = half_both(t, i) if d else half_piece(t, i, 1 - b)
+                core_copies[t, d] = sender.send(block, block, at.core_peer)
+
+    wavefront((after_z, after_y, after_x), 5)
+    target_x.wait_recv()
+    block = targets.at[at.x_peer[0]]
+    target_last = sender.send(block, block, at.core_peer)
+    for copy in core_copies.values():
+        copy.wait_recv()
+    target_core.wait_recv()
+    target_last.wait_recv()
+    sender.drain()
+    for copy in locals_:
+        copy.wait()
+
+
+def gather_all(w_in, w_out, dec_in, dec_conv, dec_out, own_targets):
+    shards, copies = lax.axis_size("fsdp"), lax.axis_size("copy")
+    groups = shards // 2
+    width, hidden = w_in.shape[0] * shards, w_in.shape[1]
+    conv_rows, layers, kernel, channels = dec_conv.shape
+    ins = (
+        w_in.reshape(2, 2, -1, w_in.shape[1]),
+        w_out.reshape(2, 2, -1, w_out.shape[1]),
+        jnp.transpose(dec_conv, (1, 2, 0, 3)),
+        dec_out,
+        dec_in.reshape(2, -1, dec_in.shape[1]),
+        own_targets.reshape(-1, own_targets.shape[-1]),
+    )
+    shapes = [(groups, 2) + ins[t].shape for t in (0, 1)]
+    shapes.append((layers, kernel, groups, 2, conv_rows, channels))
+    shapes += [(groups, 2) + ins[3].shape, (groups, 2) + ins[4].shape, (copies,) + ins[5].shape]
+    count = 5 * groups + 5 * groups + 3 * groups + 3 + 2 * groups + 3 * groups
+    sent = 2 * sum(math.prod(shape) for shape in shapes)
+    outs = pl.pallas_call(
+        lambda *refs: gather_kernel(groups, dec_out.shape[1] // 4, *refs),
+        name="gather_weights",
+        out_shape=[jax.ShapeDtypeStruct(shape, jnp.bfloat16) for shape in shapes],
+        in_specs=[pl.BlockSpec(memory_space=pltpu.VMEM)] * 6,
+        out_specs=[pl.BlockSpec(memory_space=pl.ANY)] * 6,
+        scratch_shapes=[
+            pltpu.SemaphoreType.DMA((count,)),
+            pltpu.SemaphoreType.DMA((count,)),
+            pltpu.SemaphoreType.DMA((6,)),
+        ],
+        compiler_params=pltpu.CompilerParams(
+            collective_id=0, has_side_effects=True, vmem_limit_bytes=VMEM_LIMIT
+        ),
+        cost_estimate=pl.CostEstimate(flops=0, bytes_accessed=sent, transcendentals=0),
+    )(*ins)
+    return (
+        outs[0].reshape(width, hidden),
+        outs[1].reshape(hidden, width),
+        outs[4].reshape(width, channels),
+        outs[2].reshape(layers, kernel * channels, channels),
+        outs[3].reshape(channels, width),
+        outs[5],
+    )
+
+
+def reduce_kernel(groups, quarter, w_in, w_out, conv, dec_out, dec_in, loss,
+                  w_in_sum, w_out_sum, conv_sum, dec_out_sum, dec_in_sum, loss_sum,
+                  c0, c1, c2, c3, c4, x0, x1, x3, y0, y1, y2, y3, y4, z0, z1, z2, z3, z4,
+                  f2, f4, e2, e4, lc, lcs, lx, lxs, ly, lys, lz, send_sem, recv_sem):
+    at = Place(groups)
+    a, b, h, x = at.a, at.b, at.h, at.x
+    half = 2 * quarter
+    sender = Sender(send_sem, recv_sem)
+    ins = (w_in, w_out, conv, dec_out, dec_in)
+    outs = (w_in_sum, w_out_sum, conv_sum, dec_out_sum, dec_in_sum)
+    rc, rx, ry, rz = (c0, c1, c2, c3, c4), (x0, x1, None, x3, None), (y0, y1, y2, y3, y4), (z0, z1, z2, z3, z4)
+    first, other = (None, None, f2, None, f4), (None, None, e2, None, e4)
+    split = (True, True, False, True, False)
+
+    def plus(left, right):
+        return (left.astype(jnp.float32) + right.astype(jnp.float32)).astype(jnp.bfloat16)
+
+    def each(total, body):
+        def step(i, carry):
+            body(i)
+            return carry
+
+        lax.fori_loop(0, total, step, 0)
+
+    at.greet()
+    copies = {}
+    for t in range(5):
+        if t == 2:
+            source = ins[t].at[1 - h]
+        elif t == 3:
+            source = ins[t].at[:, :, :, columns(1 - h, half)]
+        else:
+            source = ins[t].at[:, :, 1 - h]
+        copies["c", t] = sender.send(source, rc[t], at.core_peer)
+        if t == 0:
+            copies["c", 5] = sender.send(loss, lc, at.core_peer)
+
+    def after_core(t):
+        copies["c", t].wait_recv()
+        if t == 5:
+            lcs[...] = loss[...] + lc[...]
+            copies["x", t] = sender.send(lcs, lx, at.x_peer)
+            return
+        c, g = rc[t], ins[t]
+
+        def body(i):
+            if t == 2:
+                c[i] = plus(c[i], g[h, i])
+            elif t == 3:
+                c[i] = plus(c[i], g[i, :, :, columns(h, half)])
+            else:
+                c[i] = plus(c[i], g[i, :, h])
+
+        each(c.shape[0], body)
+        if t < 2:
+            copies["x", t] = sender.send(c.at[:, :, 1 - x], rx[t], at.x_peer)
+        elif t == 3:
+            copies["x", t] = sender.send(c.at[:, :, :, columns(1 - x, quarter)], rx[t], at.x_peer)
+
+    def after_x(t):
+        if t == 5:
+            copies["x", t].wait_recv()
+            lxs[...] = lcs[...] + lx[...]
+            copies["y", t] = sender.send(lxs, ly, at.y_peer)
+            return
+        current = rc[t]
+        if split[t]:
+            copies["x", t].wait_recv()
+            c, r = rc[t], rx[t]
+
+            def body(i):
+                if t == 3:
+                    r[i] = plus(r[i], c[i, :, :, columns(x, quarter)])
+                else:
+                    r[i] = plus(r[i], c[i, :, x])
+
+            each(groups, body)
+            current = r
+        source = current.at[:, :, 1 - b] if t == 2 else current.at[:, 1 - b]
+        copies["y", t] = sender.send(source, ry[t], at.y_peer)
+
+    def after_y(t):
+        copies["y", t].wait_recv()
+        if t == 5:
+            lys[...] = lxs[...] + ly[...]
+            lz[a] = lys[...]
+            for d in range(1, groups):
+                copies["z", t, d] = sender.send(lys, lz.at[a], at.z_peer(d))
+            return
+        current = rx[t] if split[t] else rc[t]
+        r = ry[t]
+
+        def body(i):
+            if t == 2:
+                r[i] = plus(r[i], current[i, :, b])
+            else:
+                r[i] = plus(r[i], current[i, b])
+
+        each(r.shape[0], body)
+        for d in range(1, groups):
+            source = r.at[:, at.later(d)] if t == 2 else r.at[at.later(d)]
+            copies["z", t, d] = sender.send(source, rz[t].at[d - 1], at.z_peer(d))
+
+    def after_z(t):
+        for d in range(1, groups):
+            copies["z", t, d].wait_recv()
+        if t == 5:
+            total = lz[0]
+            for i in range(1, groups):
+                total = total + lz[i]
+            loss_sum[...] = total
+            return
+        r = rz[t]
+        total = (ry[t][:, a] if t == 2 else ry[t][a]).astype(jnp.float32)
+        for d in range(1, groups):
+            total = total + r[d - 1].astype(jnp.float32)
+        total = total.astype(jnp.bfloat16)
+        if t < 2:
+            outs[t][h, x] = total
+            block = outs[t].at[h, x]
+            copies["e", t] = sender.send(block, block, at.x_peer)
+        elif t == 3:
+            outs[t][:, columns(2 * h + x, quarter)] = total
+            block = outs[t].at[:, columns(2 * h + x, quarter)]
+            copies["e", t] = sender.send(block, block, at.x_peer)
+        else:
+            first[t][...] = total
+            copies["e", t] = sender.send(first[t], other[t], at.x_peer)
+
+    def after_exchange(t):
+        if t == 5:
+            return
+        copies["e", t].wait_recv()
+        if not split[t]:
+            outs[t][h] = plus(first[t][...], other[t][...])
+        block = outs[t].at[:, columns(h, half)] if t == 3 else outs[t].at[h]
+        copies["f", t] = sender.send(block, block, at.core_peer)
+
+    wavefront((after_core, after_x, after_y, after_z, after_exchange), 6)
+    for t in range(5):
+        copies["f", t].wait_recv()
+    sender.drain()
+
+
+def reduce_all(in_proj, out_proj, dec_in, conv, dec_out, loss):
+    shards = lax.axis_size("fsdp")
+    groups = shards // 2
+    rows_in, rows_out, rows_dec = in_proj.shape[0] // shards, out_proj.shape[0] // shards, dec_out.shape[0] // shards
+    layers, taps, channels = conv.shape[0], conv.shape[1], conv.shape[3]
+    hidden, width = in_proj.shape[1], out_proj.shape[1]
+    quarter = width // 4
+    q_in, q_out, half_dec = rows_in // 4, rows_out // 4, rows_in // 2
+    ins = (
+        in_proj.reshape(groups, 2, 2, 2, q_in, hidden),
+        out_proj.reshape(groups, 2, 2, 2, q_out, width),
+        conv.reshape(layers, taps, groups, 2, rows_dec, channels),
+        dec_out.reshape(groups, 2, rows_dec, width),
+        dec_in.reshape(groups, 2, 2, half_dec, channels),
+        loss,
+    )
+    outs = (
+        (2, 2, q_in, hidden), (2, 2, q_out, width), (layers, taps, rows_dec, channels),
+        (rows_dec, width), (2, half_dec, channels),
+    )
+    half_shapes = (
+        (groups, 2, 2, q_in, hidden), (groups, 2, 2, q_out, width), (taps, groups, 2, rows_dec, channels),
+        (groups, 2, rows_dec, 2 * quarter), (groups, 2, half_dec, channels),
+    )
+    x_shapes = ((groups, 2, q_in, hidden), (groups, 2, q_out, width), (groups, 2, rows_dec, quarter))
+    last = ((q_in, hidden), (q_out, width), (taps, rows_dec, channels), (rows_dec, quarter), (half_dec, channels))
+    y_shapes = ((groups,) + last[0], (groups,) + last[1], (taps, groups, rows_dec, channels), (groups,) + last[3], (groups,) + last[4])
+    z_shapes = tuple((groups - 1,) + shape for shape in last)
+    scratch = half_shapes + x_shapes + y_shapes + z_shapes + (last[2], last[4], last[2], last[4])
+    count = 6 + 4 + 6 + 6 * (groups - 1) + 5 + 5
+    tile = loss.shape
+    sums = pl.pallas_call(
+        lambda *refs: reduce_kernel(groups, quarter, *refs),
+        name="reduce_grads",
+        out_shape=[jax.ShapeDtypeStruct(shape, jnp.bfloat16) for shape in outs]
+        + [jax.ShapeDtypeStruct(tile, jnp.float32)],
+        in_specs=[pl.BlockSpec(memory_space=pltpu.VMEM)] * 6,
+        out_specs=[pl.BlockSpec(memory_space=pltpu.VMEM)] * 6,
+        scratch_shapes=[pltpu.VMEM(shape, jnp.bfloat16) for shape in scratch]
+        + [pltpu.VMEM(tile, jnp.float32)] * 6
+        + [pltpu.VMEM((groups,) + tile, jnp.float32)]
+        + [pltpu.SemaphoreType.DMA((count,)), pltpu.SemaphoreType.DMA((count,))],
+        compiler_params=pltpu.CompilerParams(
+            collective_id=1, has_side_effects=True, vmem_limit_bytes=VMEM_LIMIT
+        ),
+    )(*ins)
+    return (
+        sums[0].reshape(rows_in, hidden),
+        sums[1].reshape(rows_out, width),
+        sums[4].reshape(rows_in, channels),
+        jnp.transpose(sums[2], (2, 0, 1, 3)),
+        sums[3],
+        sums[5][0, 0],
     )
 
 
@@ -51,10 +460,6 @@
     for k in range(width):
         total = total + padded[:, 2 * half - k : 2 * half - k + frames, k]
     return total
-
-
-def kernel_matrix(kernels, layer):
-    return jnp.transpose(kernels[:, layer], (1, 0, 2)).reshape(-1, kernels.shape[3])
 
 
 def teacher_targets(layer_outputs, lengths):
@@ -101,24 +506,19 @@
     rows = units * keep_count
     masked_count = frames - keep_count
     frame_index = jnp.arange(frames, dtype=jnp.int32)
-    kept_all = jnp.any(keep_index[:, :, :, None] == frame_index[None, None, None, :], axis=2)
     valid = frame_index[None, :] < lengths[:, None]
     own_keep = lax.dynamic_index_in_dim(keep_index, copy_index, 0, keepdims=False)
-    own_kept = lax.dynamic_index_in_dim(kept_all, copy_index, 0, keepdims=False)
+    chosen = own_keep[:, None, :] == frame_index[None, :, None]
+    own_kept = jnp.any(chosen, axis=2)
+    select = chosen.astype(jnp.bfloat16)
     masked = jnp.logical_and(valid, jnp.logical_not(own_kept)).astype(jnp.float32)
-    unit_index = jnp.arange(units, dtype=jnp.int32)[:, None]
     own_lengths = lax.dynamic_slice_in_dim(lengths, copy_index * per_copy, per_copy, 0)
     own_targets = teacher_targets(teacher_layers[:, 0], own_lengths)
-    targets = lax.all_gather(own_targets, "copy", axis=0, tiled=True)
     hidden_rows = student_hidden[0].reshape(rows, width).astype(jnp.float32)
     normed_exact, inv_scale = layer_norm(hidden_rows)
     normed = normed_exact.astype(jnp.bfloat16)
-    w_in_all, w_out_all, dec_in_all, dec_conv_all, dec_out_all = (
-        lax.all_gather(w_in, "fsdp", axis=0, tiled=True),
-        lax.all_gather(w_out, "fsdp", axis=0, tiled=True),
-        lax.all_gather(dec_in, "fsdp", axis=0, tiled=True),
-        lax.all_gather(dec_conv, "fsdp", axis=0, tiled=True),
-        lax.all_gather(dec_out, "fsdp", axis=0, tiled=True),
+    w_in_all, w_out_all, dec_in_all, dec_conv_all, dec_out_all, targets = gather_all(
+        w_in, w_out, dec_in, dec_conv, dec_out, own_targets
     )
     projected = jnp.dot(normed, w_in_all, preferred_element_type=jnp.float32)
     activation = gelu_value(projected).astype(jnp.bfloat16)
@@ -127,16 +527,17 @@
     lifted = jnp.dot(student_out, dec_in_all, preferred_element_type=jnp.float32).astype(
         jnp.bfloat16
     )
-    state = (
-        jnp.zeros((units, frames, channels), jnp.bfloat16)
-        .at[unit_index, own_keep]
-        .set(lifted.reshape(units, keep_count, channels))
-    )
+    state = jnp.einsum(
+        "utk,ukc->utc",
+        select,
+        lifted.reshape(units, keep_count, channels),
+        preferred_element_type=jnp.float32,
+    ).astype(jnp.bfloat16)
     saved = []
     for layer in range(layers):
         unfolded = unfold_frames(state, kernel).reshape(units * frames, kernel * channels)
         convolved = jnp.dot(
-            unfolded, kernel_matrix(dec_conv_all, layer), preferred_element_type=jnp.float32
+            unfolded, dec_conv_all[layer], preferred_element_type=jnp.float32
         )
         conv_normed, conv_scale = layer_norm(convolved)
         result = gelu_value(conv_normed)
@@ -161,7 +562,7 @@
             state_grad * gelu_slope(conv_normed), conv_normed, conv_scale
         ).astype(jnp.bfloat16)
         kernel_terms[layer] = contract_rows(unfolded, filter_grad)
-        unfold_grad = contract_cols(filter_grad, kernel_matrix(dec_conv_all, layer))
+        unfold_grad = contract_cols(filter_grad, dec_conv_all[layer])
         previous_grad = fold_frames(
             unfold_grad.reshape(units, frames, kernel * channels), kernel, channels
         ).reshape(units * frames, channels)
@@ -169,15 +570,14 @@
             previous_grad = previous_grad + state_grad
         state_grad = previous_grad
     conv_term = jnp.stack(
-        [
-            jnp.transpose(term.reshape(kernel, channels, channels), (1, 0, 2))
-            for term in kernel_terms
-        ],
-        axis=1,
+        [term.reshape(kernel, channels, channels).astype(jnp.bfloat16) for term in kernel_terms]
     )
     lifted_grad = (
-        jnp.take_along_axis(
-            state_grad.reshape(units, frames, channels), own_keep[:, :, None], axis=1
+        jnp.einsum(
+            "utk,utc->ukc",
+            select,
+            state_grad.reshape(units, frames, channels).astype(jnp.bfloat16),
+            preferred_element_type=jnp.float32,
         )
         .reshape(rows, channels)
         .astype(jnp.bfloat16)
@@ -191,47 +591,20 @@
     grad_hidden = (output_grad + norm_backward(normed_grad, normed_exact, inv_scale)).astype(
         jnp.bfloat16
     )
-    input_share = lax.psum_scatter(
+    *summed, loss_total = reduce_all(
         contract_rows(normed, projected_grad).astype(jnp.bfloat16),
-        "fsdp",
-        scatter_dimension=0,
-        tiled=True,
-    )
-    output_share = lax.psum_scatter(
         contract_rows(activation, output_half).astype(jnp.bfloat16),
-        "fsdp",
-        scatter_dimension=0,
-        tiled=True,
-    )
-    decoder_in_share, decoder_conv_share, decoder_out_share = (
-        lax.psum_scatter(
-            in_term.astype(jnp.bfloat16), "fsdp", scatter_dimension=0, tiled=True
-        ).astype(jnp.float32),
-        lax.psum_scatter(
-            conv_term.astype(jnp.bfloat16), "fsdp", scatter_dimension=0, tiled=True
-        ).astype(jnp.float32),
-        lax.psum_scatter(
-            out_term.astype(jnp.bfloat16), "fsdp", scatter_dimension=0, tiled=True
-        ).astype(jnp.float32),
-    )
-    summed = (
-        lax.psum(input_share, "copy").astype(jnp.float32),
-        lax.psum(output_share, "copy").astype(jnp.float32),
-        lax.psum(decoder_in_share.astype(jnp.bfloat16), "copy").astype(jnp.float32),
-        lax.psum(decoder_conv_share.astype(jnp.bfloat16), "copy").astype(jnp.float32),
-        lax.psum(decoder_out_share.astype(jnp.bfloat16), "copy").astype(jnp.float32),
-    )
-    loss_total = lax.psum(total, ("copy", "fsdp"))
+        in_term.astype(jnp.bfloat16),
+        conv_term,
+        out_term.astype(jnp.bfloat16),
+        jnp.full((8, 128), total, jnp.float32),
+    )
     slot_total = lax.axis_size("copy") * lax.axis_size("fsdp") * units * masked_count
     loss = loss_total / float(slot_total)
     return (
         loss,
         grad_hidden.reshape(1, units, keep_count, width),
-        summed[0].astype(jnp.bfloat16),
-        summed[1].astype(jnp.bfloat16),
-        summed[2].astype(jnp.bfloat16),
-        summed[3].astype(jnp.bfloat16),
-        summed[4].astype(jnp.bfloat16),
+        *summed,
     )
 
 

time: 779 us -> 327 us (0.42)
  waiting for transfers between devices: 499 us -> 0 us
  Pallas kernels: 0 us -> 215 us
  blocking collectives: 101 us -> 0 us
  local copies, waits for them, and re-layouts: 63.5 us -> 33 us
  matrix products: 62.8 us -> 48.1 us
  between operations: 17.4 us -> 4.02 us
    reduce_scatter x5 -> x0, waiting for transfers between devices: 340 us -> none  [the longest x1 91.8 us: on_device(): lax.psum_scatter(contract_rows(activation, output_half).astype(jnp.bfloat...]
    pallas_call x0 -> x2, Pallas kernels: none -> 215 us  [the longest x1 139 us: reduce_all(): pl.pallas_call(lambda *refs: reduce_kernel(groups, quarter, *refs), name=...]
    all_gather x4 -> x0, waiting for transfers between devices: 158 us -> none  [the longest x1 68.5 us: on_device(): lax.all_gather(w_in, 'fsdp', axis=0, tiled=True)]
    all_gather x2 -> x0, blocking collectives: 60.2 us -> none  [the longest x1 32.5 us: on_device(): lax.all_gather(dec_out, 'fsdp', axis=0, tiled=True)]
    psum x1 -> x0, blocking collectives: 40.8 us -> none  [on_device(): loss_total = lax.psum(total, ('copy', 'fsdp'))]
    scatter x1 -> x0, local copies, waits for them, and re-layouts: 22.3 us -> none  [on_device(): state = jnp.zeros((units, frames, channels), jnp.bfloat16).at[unit_index,...]
    dot_general x6, matrix products: 23.1 us -> 11.8 us  [contract_cols(): lax.dot_general(left, right, (((1,), (1,)), ((), ())), preferred_element_...]
    unnamed x72 -> x84, local copies, waits for them, and re-layouts: 18.2 us -> 13.4 us
  transfers between devices with their start and end apart: 10 -> 0, of which waited for: 7 -> 0; matrix products, arithmetic and copies ran while one was open for 16% -> 0% of each run, Pallas kernels for 0% -> 0%
where the time goes in v1:
time: 327 us; the launch traced here: 321 us
  Pallas kernels  215 us (66%)
  matrix products  48.1 us (15%)
  local copies, waits for them, and re-layouts  33 us (10%)
  other arithmetic  20.5 us (6%)
  between operations  4.02 us (1%)
    pallas_call x1, Pallas kernels, reduce_all(): pl.pallas_call(lambda *refs: reduce_kernel(groups, quarter, *refs), name=...  139 us
    pallas_call x1, Pallas kernels, gather_all(): pl.pallas_call(lambda *refs: gather_kernel(groups, dec_out.shape[1] // 4,...  76.5 us
    dot_general x6, matrix products, contract_rows(): lax.dot_general(left, right, (((0,), (0,)), ((), ())), preferred_element_...  18.5 us
    unnamed x84, local copies, waits for them, and re-layouts  13.4 us
    dot_general x6, matrix products, contract_cols(): lax.dot_general(left, right, (((1,), (1,)), ((), ())), preferred_element_...  11.8 us

profile of v1, /device:TPU:9, one launch (start us, length us, event | category | flops | bytes accessed | tf_op | source)
XLA Modules:
  0.0 320.8 jit_solution(6118590216338371161)
XLA Ops:
  0.7 1.4 dynamic_slice.8
  2.0 1.2 fusion.93
  3.3 0.6 compare_convert_fusion.1
  4.1 1.3 convert_reduce_fusion
  5.5 1.5 fusion.9
  7.4 0.7 broadcast_divide_fusion.3
  8.5 0.7 broadcast_divide_fusion.2
  9.2 0.7 broadcast_divide_fusion.1
  9.8 0.7 broadcast_divide_fusion
  11.0 0.7 add_rsqrt_fusion.4
  11.7 0.7 add_rsqrt_fusion.2
  12.4 1.2 fusion.63.refs_5_
  13.6 0.9 copy.30
  14.7 76.5 %gather_weights.1 = (bf16[4,2,2,2,32,2048]{5,4,3,2,1,0:T(8,128)(2,1)}, bf16[4,2,2,2,64,1024]{5,4,3,2,1,0:T(8,128)(2,1)}, bf16[2,7,4,2,48,384]{5,4,3,2,1,0:T(8,12...) custom-call(bf16[2,2,32,2048]{3,2,1,0:T(8,128)(2,1)} %bitcast.259, ...), custom_call_target="tpu_custom_call" | custom-call | bytes 15663104 | tf_op jit(solution)/shard_map/gather_weights/pallas_call | solution.py:221
  91.2 6.3 %multiply_convert_fusion.1 = (bf16[384,2048]{1,0:T(8,128)(2,1)S(1)}, f32[384,2048]{1,0:T(8,128)}) fusion(bf16[384,1024]{1,0:T(8,128)(2,1)S(1)} %bitcast.251, bf16[1024,2048]{1,0:T(8,128)(2,1)} %bitcast.267), kind=kOutput, calls=%fused_computation.26 | convolution fusion | flops 1614544896 | bytes 9699328 | tf_op jit(solution)/shard_map/dot_general | solution.py:523
  97.5 1.8 fusion.20
  101.7 1.9 copy-done.8
  103.6 6.5 %copy.23 = bf16[2688,768]{1,0:T(8,128)(2,1)} copy(bf16[2688,768]{0,1:T(8,128)(2,1)} %bitcast.238) | data formatting | bytes 8257536 | tf_op jit(solution)/shard_map/dot_general | solution.py:481
  110.1 2.8 fusion.100
  113.5 2.4 fusion.101
  117.9 2.4 fusion.102
  120.4 6.5 %copy.24 = bf16[768,2688]{0,1:T(8,128)(2,1)} copy(bf16[768,2688]{1,0:T(8,128)(2,1)} %bitcast.241) | data formatting | bytes 8257536 | tf_op jit(solution)/shard_map/reshape | solution.py:538
  127.2 1.0 add_convert_fusion
  128.8 2.9 multiply_reduce_fusion
  132.9 3.5 %convolution_convert_fusion.4 = bf16[384,1024]{1,0:T(8,128)(2,1)} fusion(bf16[768,384]{1,0:T(8,128)(2,1)} %copy-done.15, bf16[768,1024]{1,0:T(8,128)(2,1)} %get-tuple-element.61), kind=kOutput, calls=%fused_computation.50 | convolution fusion | flops 604372992 | bytes 2949120 | tf_op jit(solution)/shard_map/dot_general | solution.py:481
  136.4 1.5 fusion.97
  138.6 2.3 convolution_convert_fusion.2
  141.0 2.4 fusion.103
  143.3 0.7 fusion.36
  144.1 1.5 fusion.96
  146.2 2.3 convolution_convert_fusion.3
  148.6 2.4 pad_maximum_fusion.refs_2_
  151.0 2.4 fusion.104
  153.4 0.9 convolution_convert_fusion.7
  154.3 1.6 convolution_convert_fusion.5
  156.5 0.8 copy-done.32
  157.3 3.0 fusion.5
  160.3 2.0 fusion.95
  162.3 1.5 fusion.19
  163.8 4.4 %convolution_convert_fusion = bf16[2048,1024]{1,0:T(8,128)(2,1)} fusion(bf16[384,2048]{1,0:T(8,128)(2,1)S(1)} %copy-done.31, f32[384,1024]{1,0:T(8,128)S(1)} %fusion.105), kind=kOutput, calls=%fused_computation.14 | convolution fusion | flops 1613103104 | bytes 7340032 | tf_op jit(solution)/shard_map/dot_general | solution.py:481
  168.1 4.3 %convolution_convert_fusion.1 = bf16[1024,2048]{1,0:T(8,128)(2,1)} fusion(bf16[384,1024]{1,0:T(8,128)(2,1)S(1)} %get-tuple-element.65, bf16[384,2048]{1,0:T(8,128)(2,1)S(1)} %fusion.5), kind=kOutput, calls=%fused_computation.15 | convolution fusion | flops 1612709888 | bytes 6553600 | tf_op jit(solution)/shard_map/dot_general | solution.py:481
  172.5 138.7 %reduce_grads.1 = (bf16[2,2,32,2048]{3,2,1,0:T(8,128)(2,1)}, bf16[2,2,64,1024]{3,2,1,0:T(8,128)(2,1)}, bf16[2,7,48,384]{3,2,1,0:T(8,128)(2,1)}, bf16[48,1024]{1,...) custom-call(bf16[4,2,2,2,32,2048]{5,4,3,2,1,0:T(8,128)(2,1)} %bitcast.243, ...), custom_call_target="tpu_custom_call" | custom-call | tf_op jit(solution)/shard_map/reduce_grads/pallas_call | solution.py:422
  311.2 1.2 slice.143
  313.2 2.3 copy.25
  315.4 1.9 copy.47
  317.3 0.8 copy.48
  318.1 0.6 copy.49
  318.7 0.6 copy.50
  (109 shorter events, 10.0 us)
Async XLA Ops:
  0.6 3.3 %copy-start = (s32[4,4,96]{2,1,0:T(4,128)S(1)}, s32[4,4,96]{2,1,0:T(4,128)}, u32[]{:S(2)}) copy-start(s32[4,4,96]{2,1,0:T(4,128)} %param.10) | copy-start | bytes 18436
  0.6 6.6 %copy-start.2 = (bf16[4,1,1,192,1024]{4,3,2,1,0:T(8,128)(2,1)S(1)}, bf16[4,1,1,192,1024]{4,3,2,1,0:T(8,128)(2,1)}, u32[]{:S(2)}) copy-start(bf16[4,1,1,192,1024]{4,3,2,1,0:T(8,128)(2,1)} %param.12) | copy-start | bytes 4718596
  0.7 6.5 %copy-start.20 = (s32[4]{0:T(128)S(1)}, s32[4]{0:T(128)}, u32[]{:S(2)}) copy-start(s32[4]{0:T(128)} %param.11) | copy-start | bytes 52
  10.5 3.1 copy-start.17
  10.9 3.5 %copy-start.3 = (bf16[1,4,96,1024]{3,2,1,0:T(8,128)(2,1)S(1)}, bf16[1,4,96,1024]{3,2,1,0:T(8,128)(2,1)}, u32[]{:S(2)}) copy-start(bf16[1,4,96,1024]{3,2,1,0:T(8,128)(2,1)} %param.9) | copy-start | bytes 2359300
  91.2 6.3 %copy-start.22 = (bf16[4,2,2,2,64,1024]{5,4,3,2,1,0:T(8,128)(2,1)S(1)}, bf16[4,2,2,2,64,1024]{5,4,3,2,1,0:T(8,128)(2,1)}, u32[]{:S(2)}) copy-start(bf16[4,2,2,2,64,1024]{5,4,3,2,1,0:T(8,128)(2,1)} %get-tuple-element.20) | copy-start | bytes 12582916
  97.5 1.8 copy-start.30
  97.5 1.8 copy-start.13
  99.3 1.3 copy-start.27
  101.7 1.9 copy-start.8
  110.1 3.4 %copy-start.9 = (bf16[4,192,2688]{2,1,0:T(8,128)(2,1)S(1)}, bf16[4,192,2688]{2,1,0:T(8,128)(2,1)}, u32[]{:S(2)}) copy-start(bf16[4,192,2688]{2,1,0:T(8,128)(2,1)} %copy-done.8) | copy-start | bytes 12386308
  112.9 3.1 copy-start.4
  112.9 5.0 %copy-start.6 = (bf16[1,7,4,2,48,384]{5,4,3,2,1,0:T(8,128)(2,1)}, bf16[1,7,4,2,48,384]{5,4,3,2,1,0:T(8,128)(2,1)S(1)}, u32[]{:S(2)}) copy-start(bf16[1,7,4,2,48,384]{5,4,3,2,1,0:T(8,128)(2,1)S(1)} %get-tuple-element.62) | copy-start | bytes 6193156
  117.9 2.4 copy-start.10
  127.1 1.4 copy-start.24
  127.2 1.6 copy-start.25
  128.8 2.9 copy-start.15
  132.9 3.5 %copy-start.26 = (bf16[4,2,48,1024]{3,2,1,0:T(8,128)(2,1)S(1)}, bf16[4,2,48,1024]{3,2,1,0:T(8,128)(2,1)}, u32[]{:S(2)}) copy-start(bf16[4,2,48,1024]{3,2,1,0:T(8,128)(2,1)} %get-tuple-element.23) | copy-start | bytes 2359300
  132.9 3.5 %copy-start.29 = (bf16[768,1024]{1,0:T(8,128)(2,1)S(1)}, bf16[768,1024]{1,0:T(8,128)(2,1)}, u32[]{:S(2)}) copy-start(bf16[768,1024]{1,0:T(8,128)(2,1)} %get-tuple-element.61) | copy-start | bytes 4718596
  136.4 2.2 copy-start.12
  138.6 2.4 copy-start.7
  144.0 2.2 copy-start.11
  148.6 2.4 copy-start.5
  151.0 3.3 %copy-start.28 = (bf16[384,1024]{1,0:T(8,128)(2,1)S(1)}, bf16[384,1024]{1,0:T(8,128)(2,1)}, u32[]{:S(2)}) copy-start(bf16[384,1024]{1,0:T(8,128)(2,1)} %copy-done.27) | copy-start | bytes 2359300
  153.4 3.1 copy-start.23
  154.3 1.6 copy-start.14
  154.3 3.0 copy-start.32
  157.3 3.0 copy-start.21
  162.3 1.5 copy-start.31
  311.2 6.1 %copy-start.16 = (bf16[2,2,64,1024]{3,2,1,0:T(8,128)(2,1)S(1)}, bf16[2,2,64,1024]{3,2,1,0:T(8,128)(2,1)}, u32[]{:S(2)}) copy-start(bf16[2,2,64,1024]{3,2,1,0:T(8,128)(2,1)} %get-tuple-element.27) | copy-start | bytes 1572868
  311.2 6.9 %copy-start.19 = (bf16[2,64,384]{2,1,0:T(8,128)(2,1)S(1)}, bf16[2,64,384]{2,1,0:T(8,128)(2,1)}, u32[]{:S(2)}) copy-start(bf16[2,64,384]{2,1,0:T(8,128)(2,1)} %get-tuple-element.28) | copy-start | bytes 294916
  313.1 6.2 %copy-start.1 = (s32[4,4,96]{2,1,0:T(4,128)S(1)}, s32[4,4,96]{2,1,0:T(4,128)}, u32[]{:S(2)}) copy-start(s32[4,4,96]{2,1,0:T(4,128)} %param.10) | copy-start | bytes 18436
  313.2 5.6 %copy-start.18 = (bf16[48,1024]{1,0:T(8,128)(2,1)S(1)}, bf16[48,1024]{1,0:T(8,128)(2,1)}, u32[]{:S(2)}) copy-start(bf16[48,1024]{1,0:T(8,128)(2,1)} %get-tuple-element.91) | copy-start | bytes 294916

commit v2 on v1

--- a/solution.py
+++ b/solution.py
@@ -98,10 +98,10 @@
 
 
 def wavefront(stages, count):
-    for step in range(count + len(stages) - 1):
-        for number, stage in reversed(list(enumerate(stages))):
-            if 0 <= step - number < count:
-                stage(step - number)
+    for step in range(count + stages[-1][0]):
+        for lag, stage in reversed(stages):
+            if 0 <= step - lag < count:
+                stage(step - lag)
 
 
 def gather_kernel(groups, quarter, w_in, w_out, conv, dec_out, dec_in, own_targets,
@@ -154,40 +154,46 @@
     locals_.append(pltpu.make_async_copy(own_targets, targets.at[at.copy], local_sem.at[5]))
     for copy in locals_:
         copy.start()
+    order = (0, 2, 1, 3, 4)
+    chunks = [(t, d) for d in range(groups) for t in order]
     z_copies, y_copies, x_copies, core_copies = {}, {}, {}, {}
-    for t in range(5):
-        for d in range(1, groups):
+    for t in order:
+        y_copies[t, 0] = sender.send(own[t], piece(t, a, b), at.y_peer)
+        if groups > 1:
+            z_copies[t, 1] = sender.send(own[t], piece(t, a, b), at.z_peer(1))
+    for t, d in chunks:
+        if d > 1:
             z_copies[t, d] = sender.send(own[t], piece(t, a, b), at.z_peer(d))
-        y_copies[t, 0] = sender.send(own[t], piece(t, a, b), at.y_peer)
     target_x = sender.send(own_targets, targets.at[at.copy], at.x_peer)
     target_core = sender.send(own_targets, targets.at[at.copy], at.core_peer)
 
-    def after_z(t):
-        for d in range(1, groups):
+    def after_z(c):
+        t, d = chunks[c]
+        if d:
             z_copies[t, d].wait_recv()
             block = piece(t, at.earlier(d), b)
             y_copies[t, d] = sender.send(block, block, at.y_peer)
 
-    def after_y(t):
-        for d in range(groups):
-            y_copies[t, d].wait_recv()
+    def after_y(c):
+        t, d = chunks[c]
+        y_copies[t, d].wait_recv()
+        i = at.earlier(d)
+        if split[t]:
+            block = both(t, i) if d else piece(t, i, 1 - b)
+            x_copies[t, d] = sender.send(block, block, at.x_peer)
+        else:
+            block = half_both(t, i) if d else half_piece(t, i, 1 - b)
+            core_copies[t, d] = sender.send(block, block, at.core_peer)
+
+    def after_x(c):
+        t, d = chunks[c]
+        if split[t]:
+            x_copies[t, d].wait_recv()
             i = at.earlier(d)
-            if split[t]:
-                block = both(t, i) if d else piece(t, i, 1 - b)
-                x_copies[t, d] = sender.send(block, block, at.x_peer)
-            else:
-                block = half_both(t, i) if d else half_piece(t, i, 1 - b)
-                core_copies[t, d] = sender.send(block, block, at.core_peer)
-
-    def after_x(t):
-        if split[t]:
-            for d in range(groups):
-                x_copies[t, d].wait_recv()
-                i = at.earlier(d)
-                block = half_both(t, i) if d else half_piece(t, i, 1 - b)
-                core_copies[t, d] = sender.send(block, block, at.core_peer)
-
-    wavefront((after_z, after_y, after_x), 5)
+            block = half_both(t, i) if d else half_piece(t, i, 1 - b)
+            core_copies[t, d] = sender.send(block, block, at.core_peer)
+
+    wavefront(((0, after_z), (3, after_y), (6, after_x)), len(chunks))
     target_x.wait_recv()
     block = targets.at[at.x_peer[0]]
     target_last = sender.send(block, block, at.core_peer)
@@ -268,98 +274,122 @@
 
         lax.fori_loop(0, total, step, 0)
 
+    distances = tuple(range(1, groups)) + (0,)
+    chunks = [(t, d) for part in ((0, 2), (1, 3, 4)) for d in distances for t in part]
+    chunks.insert(2, (5, 0))
     at.greet()
     copies = {}
-    for t in range(5):
+    for t, d in chunks:
+        i = at.later(d)
+        if t == 5:
+            copies["c", t, d] = sender.send(loss, lc, at.core_peer)
+        elif t == 2:
+            copies["c", t, d] = sender.send(ins[t].at[1 - h, :, i], rc[t].at[:, i], at.core_peer)
+        elif t == 3:
+            source = ins[t].at[i, :, :, columns(1 - h, half)]
+            copies["c", t, d] = sender.send(source, rc[t].at[i], at.core_peer)
+        else:
+            copies["c", t, d] = sender.send(ins[t].at[i, :, 1 - h], rc[t].at[i], at.core_peer)
+
+    def send_y(t, d):
+        i = at.later(d)
+        current = rx[t] if split[t] else rc[t]
         if t == 2:
-            source = ins[t].at[1 - h]
-        elif t == 3:
-            source = ins[t].at[:, :, :, columns(1 - h, half)]
+            copies["y", t, d] = sender.send(current.at[:, i, 1 - b], ry[t].at[:, i], at.y_peer)
         else:
-            source = ins[t].at[:, :, 1 - h]
-        copies["c", t] = sender.send(source, rc[t], at.core_peer)
-        if t == 0:
-            copies["c", 5] = sender.send(loss, lc, at.core_peer)
-
-    def after_core(t):
-        copies["c", t].wait_recv()
+            copies["y", t, d] = sender.send(current.at[i, 1 - b], ry[t].at[i], at.y_peer)
+
+    def after_core(index):
+        t, d = chunks[index]
+        copies["c", t, d].wait_recv()
         if t == 5:
             lcs[...] = loss[...] + lc[...]
-            copies["x", t] = sender.send(lcs, lx, at.x_peer)
+            copies["x", t, d] = sender.send(lcs, lx, at.x_peer)
             return
-        c, g = rc[t], ins[t]
-
-        def body(i):
-            if t == 2:
-                c[i] = plus(c[i], g[h, i])
-            elif t == 3:
-                c[i] = plus(c[i], g[i, :, :, columns(h, half)])
+        c, g, i = rc[t], ins[t], at.later(d)
+        if t < 2:
+
+            def body(k):
+                j, q = k // 2, k % 2
+                c[i, j, q] = plus(c[i, j, q], g[i, j, h, q])
+
+            each(4, body)
+            copies["x", t, d] = sender.send(c.at[i, :, 1 - x], rx[t].at[i], at.x_peer)
+        elif t == 2:
+
+            def body(k):
+                c[k, i] = plus(c[k, i], g[h, k, i])
+
+            each(c.shape[0], body)
+            send_y(t, d)
+        elif t == 3:
+            c[i] = plus(c[i], g[i, :, :, columns(h, half)])
+            source = c.at[i, :, :, columns(1 - x, quarter)]
+            copies["x", t, d] = sender.send(source, rx[t].at[i], at.x_peer)
+        else:
+            c[i] = plus(c[i], g[i, :, h])
+            send_y(t, d)
+
+    def after_x(index):
+        t, d = chunks[index]
+        if t == 5:
+            copies["x", t, d].wait_recv()
+            lxs[...] = lcs[...] + lx[...]
+            copies["y", t, d] = sender.send(lxs, ly, at.y_peer)
+        elif split[t]:
+            copies["x", t, d].wait_recv()
+            c, r, i = rc[t], rx[t], at.later(d)
+            if t == 3:
+                r[i] = plus(r[i], c[i, :, :, columns(x, quarter)])
             else:
-                c[i] = plus(c[i], g[i, :, h])
-
-        each(c.shape[0], body)
-        if t < 2:
-            copies["x", t] = sender.send(c.at[:, :, 1 - x], rx[t], at.x_peer)
-        elif t == 3:
-            copies["x", t] = sender.send(c.at[:, :, :, columns(1 - x, quarter)], rx[t], at.x_peer)
-
-    def after_x(t):
-        if t == 5:
-            copies["x", t].wait_recv()
-            lxs[...] = lcs[...] + lx[...]
-            copies["y", t] = sender.send(lxs, ly, at.y_peer)
-            return
-        current = rc[t]
-        if split[t]:
-            copies["x", t].wait_recv()
-            c, r = rc[t], rx[t]
-
-            def body(i):
-                if t == 3:
-                    r[i] = plus(r[i], c[i, :, :, columns(x, quarter)])
-                else:
-                    r[i] = plus(r[i], c[i, :, x])
-
-            each(groups, body)
-            current = r
-        source = current.at[:, :, 1 - b] if t == 2 else current.at[:, 1 - b]
-        copies["y", t] = sender.send(source, ry[t], at.y_peer)
-
-    def after_y(t):
-        copies["y", t].wait_recv()
+
+                def body(k):
+                    r[i, k] = plus(r[i, k], c[i, k, x])
+
+                each(2, body)
+            send_y(t, d)
+
+    def after_y(index):
+        t, d = chunks[index]
+        copies["y", t, d].wait_recv()
         if t == 5:
             lys[...] = lxs[...] + ly[...]
             lz[a] = lys[...]
-            for d in range(1, groups):
-                copies["z", t, d] = sender.send(lys, lz.at[a], at.z_peer(d))
+            for e in range(1, groups):
+                copies["z", t, e] = sender.send(lys, lz.at[a], at.z_peer(e))
             return
         current = rx[t] if split[t] else rc[t]
-        r = ry[t]
-
-        def body(i):
-            if t == 2:
-                r[i] = plus(r[i], current[i, :, b])
-            else:
-                r[i] = plus(r[i], current[i, b])
-
-        each(r.shape[0], body)
-        for d in range(1, groups):
-            source = r.at[:, at.later(d)] if t == 2 else r.at[at.later(d)]
+        r, i = ry[t], at.later(d)
+        if t == 2:
+
+            def body(k):
+                r[k, i] = plus(r[k, i], current[k, i, b])
+
+            each(r.shape[0], body)
+        else:
+            r[i] = plus(r[i], current[i, b])
+        if d:
+            source = r.at[:, i] if t == 2 else r.at[i]
             copies["z", t, d] = sender.send(source, rz[t].at[d - 1], at.z_peer(d))
 
-    def after_z(t):
-        for d in range(1, groups):
-            copies["z", t, d].wait_recv()
+    def after_z(index):
+        t, d = chunks[index]
         if t == 5:
+            for e in range(1, groups):
+                copies["z", t, e].wait_recv()
             total = lz[0]
             for i in range(1, groups):
                 total = total + lz[i]
             loss_sum[...] = total
             return
+        if d:
+            return
+        for e in range(1, groups):
+            copies["z", t, e].wait_recv()
         r = rz[t]
         total = (ry[t][:, a] if t == 2 else ry[t][a]).astype(jnp.float32)
-        for d in range(1, groups):
-            total = total + r[d - 1].astype(jnp.float32)
+        for e in range(1, groups):
+            total = total + r[e - 1].astype(jnp.float32)
         total = total.astype(jnp.bfloat16)
         if t < 2:
             outs[t][h, x] = total
@@ -373,8 +403,9 @@
             first[t][...] = total
             copies["e", t] = sender.send(first[t], other[t], at.x_peer)
 
-    def after_exchange(t):
-        if t == 5:
+    def after_exchange(index):
+        t, d = chunks[index]
+        if t == 5 or d:
             return
         copies["e", t].wait_recv()
         if not split[t]:
@@ -382,7 +413,9 @@
         block = outs[t].at[:, columns(h, half)] if t == 3 else outs[t].at[h]
         copies["f", t] = sender.send(block, block, at.core_peer)
 
-    wavefront((after_core, after_x, after_y, after_z, after_exchange), 6)
+    wavefront(
+        ((0, after_core), (2, after_x), (4, after_y), (6, after_z), (8, after_exchange)), len(chunks)
+    )
     for t in range(5):
         copies["f", t].wait_recv()
     sender.drain()
@@ -417,7 +450,7 @@
     y_shapes = ((groups,) + last[0], (groups,) + last[1], (taps, groups, rows_dec, channels), (groups,) + last[3], (groups,) + last[4])
     z_shapes = tuple((groups - 1,) + shape for shape in last)
     scratch = half_shapes + x_shapes + y_shapes + z_shapes + (last[2], last[4], last[2], last[4])
-    count = 6 + 4 + 6 + 6 * (groups - 1) + 5 + 5
+    count = (5 + 3 + 5) * groups + 3 + 6 * (groups - 1) + 5 + 5
     tile = loss.shape
     sums = pl.pallas_call(
         lambda *refs: reduce_kernel(groups, quarter, *refs),

time: 327 us -> 295 us (0.902)
  Pallas kernels: 215 us -> 185 us
    pallas_call x1, Pallas kernels: 139 us -> 111 us  [reduce_all(): pl.pallas_call(lambda *refs: reduce_kernel(groups, quarter, *refs), name=...]
where the time goes in v2:
time: 295 us; the launch traced here: 291 us
  Pallas kernels  185 us (63%)
  matrix products  48.1 us (16%)
  local copies, waits for them, and re-layouts  33 us (11%)
  other arithmetic  20.5 us (7%)
  between operations  4.02 us (1%)
    pallas_call x1, Pallas kernels, reduce_all(): pl.pallas_call(lambda *refs: reduce_kernel(groups, quarter, *refs), name=...  111 us
    pallas_call x1, Pallas kernels, gather_all(): pl.pallas_call(lambda *refs: gather_kernel(groups, dec_out.shape[1] // 4,...  74.4 us
    dot_general x6, matrix products, contract_rows(): lax.dot_general(left, right, (((0,), (0,)), ((), ())), preferred_element_...  18.5 us
    unnamed x84, local copies, waits for them, and re-layouts  13.4 us
    dot_general x6, matrix products, contract_cols(): lax.dot_general(left, right, (((1,), (1,)), ((), ())), preferred_element_...  11.8 us
    dot_general x1, local copies, waits for them, and re-layouts, contract_rows(): lax.dot_general(left, right, (((0,), (0,)), ((), ())), preferred_element_...  6.51 us
    reshape x1, local copies, waits for them, and re-layouts, on_device(): unfold_frames(state, kernel).reshape(units * frames, kernel * channels)  6.49 us
    dot_general x1, matrix products, on_device(): projected = jnp.dot(normed, w_in_all, preferred_element_type=jnp.float32)  6.29 us

profile of v2, /device:TPU:9, one launch (start us, length us, event | category | flops | bytes accessed | tf_op | source)
XLA Modules:
  0.0 290.7 jit_solution(7582546015445281845)
XLA Ops:
  0.7 1.4 dynamic_slice.8
  2.0 1.2 fusion.93
  3.3 0.6 compare_convert_fusion.1
  4.1 1.3 convert_reduce_fusion
  5.5 1.5 fusion.9
  7.4 0.7 broadcast_divide_fusion.3
  8.5 0.7 broadcast_divide_fusion.2
  9.2 0.7 broadcast_divide_fusion.1
  9.8 0.7 broadcast_divide_fusion
  11.0 0.7 add_rsqrt_fusion.4
  11.7 0.7 add_rsqrt_fusion.2
  12.4 1.2 fusion.63.refs_5_
  13.6 0.9 copy.30
  14.7 74.4 %gather_weights.1 = (bf16[4,2,2,2,32,2048]{5,4,3,2,1,0:T(8,128)(2,1)}, bf16[4,2,2,2,64,1024]{5,4,3,2,1,0:T(8,128)(2,1)}, bf16[2,7,4,2,48,384]{5,4,3,2,1,0:T(8,12...) custom-call(bf16[2,2,32,2048]{3,2,1,0:T(8,128)(2,1)} %bitcast.259, ...), custom_call_target="tpu_custom_call" | custom-call | bytes 15663104 | tf_op jit(solution)/shard_map/gather_weights/pallas_call | solution.py:227
  89.1 6.3 %multiply_convert_fusion.1 = (bf16[384,2048]{1,0:T(8,128)(2,1)S(1)}, f32[384,2048]{1,0:T(8,128)}) fusion(bf16[384,1024]{1,0:T(8,128)(2,1)S(1)} %bitcast.251, bf16[1024,2048]{1,0:T(8,128)(2,1)} %bitcast.267), kind=kOutput, calls=%fused_computation.26 | convolution fusion | flops 1614544896 | bytes 9699328 | tf_op jit(solution)/shard_map/dot_general | solution.py:556
  95.4 1.8 fusion.20
  99.6 1.9 copy-done.8
  101.5 6.5 %copy.23 = bf16[2688,768]{1,0:T(8,128)(2,1)} copy(bf16[2688,768]{0,1:T(8,128)(2,1)} %bitcast.238) | data formatting | bytes 8257536 | tf_op jit(solution)/shard_map/dot_general | solution.py:514
  108.1 2.8 fusion.100
  111.5 2.4 fusion.101
  115.9 2.4 fusion.102
  118.3 6.5 %copy.24 = bf16[768,2688]{0,1:T(8,128)(2,1)} copy(bf16[768,2688]{1,0:T(8,128)(2,1)} %bitcast.241) | data formatting | bytes 8257536 | tf_op jit(solution)/shard_map/reshape | solution.py:571
  125.1 1.0 add_convert_fusion
  126.7 2.9 %multiply_reduce_fusion = (f32[]{:T(128)}, bf16[768,1024]{1,0:T(8,128)(2,1)}) fusion(bf16[4,192,1024]{2,1,0:T(8,128)(2,1)S(1)} %copy-done.24, f32[768]{0:T(1024)S(1)} %reshape.889, bf16[768,384]{1,0:T(8,128)(2,1)S(1)} %add_convert_fusion, bf16[384,1024]{1,0:T(8,128)(2,1)S(1)} %bitcast.271), kind=kOutput, calls=%fused_computation.24 | convolution fusion | flops 609484800 | bytes 4525060 | tf_op jit(solution)/shard_map/dot_general | solution.py:582
  130.9 3.5 %convolution_convert_fusion.4 = bf16[384,1024]{1,0:T(8,128)(2,1)} fusion(bf16[768,384]{1,0:T(8,128)(2,1)} %copy-done.15, bf16[768,1024]{1,0:T(8,128)(2,1)} %get-tuple-element.61), kind=kOutput, calls=%fused_computation.50 | convolution fusion | flops 604372992 | bytes 2949120 | tf_op jit(solution)/shard_map/dot_general | solution.py:514
  134.4 1.5 fusion.97
  136.5 2.3 convolution_convert_fusion.2
  138.9 2.4 fusion.103
  141.3 0.7 fusion.36
  142.0 1.5 fusion.96
  144.2 2.3 convolution_convert_fusion.3
  146.5 2.4 pad_maximum_fusion.refs_2_
  148.9 2.4 fusion.104
  151.3 0.9 convolution_convert_fusion.7
  152.2 1.6 convolution_convert_fusion.5
  154.5 0.8 copy-done.32
  155.2 3.0 %fusion.5 = bf16[384,2048]{1,0:T(8,128)(2,1)S(1)} fusion(f32[384,2048]{1,0:T(8,128)S(1)} %copy-done.32, bf16[2048,1024]{1,0:T(8,128)(2,1)S(1)} %bitcast.270, f32[384,1024]{1,0:T(8,128)S(1)} %fusion.105), kind=kOutput, calls=%fused_computation.21 | convolution fusion | flops 1618870272 | bytes 10485760 | tf_op jit(solution)/shard_map/dot_general | solution.py:520
  158.2 2.0 fusion.95
  160.3 1.5 fusion.19
  161.7 4.4 %convolution_convert_fusion = bf16[2048,1024]{1,0:T(8,128)(2,1)} fusion(bf16[384,2048]{1,0:T(8,128)(2,1)S(1)} %copy-done.31, f32[384,1024]{1,0:T(8,128)S(1)} %fusion.105), kind=kOutput, calls=%fused_computation.14 | convolution fusion | flops 1613103104 | bytes 7340032 | tf_op jit(solution)/shard_map/dot_general | solution.py:514
  166.1 4.3 %convolution_convert_fusion.1 = bf16[1024,2048]{1,0:T(8,128)(2,1)} fusion(bf16[384,1024]{1,0:T(8,128)(2,1)S(1)} %get-tuple-element.65, bf16[384,2048]{1,0:T(8,128)(2,1)S(1)} %fusion.5), kind=kOutput, calls=%fused_computation.15 | convolution fusion | flops 1612709888 | bytes 6553600 | tf_op jit(solution)/shard_map/dot_general | solution.py:514
  170.4 110.8 %reduce_grads.1 = (bf16[2,2,32,2048]{3,2,1,0:T(8,128)(2,1)}, bf16[2,2,64,1024]{3,2,1,0:T(8,128)(2,1)}, bf16[2,7,48,384]{3,2,1,0:T(8,128)(2,1)}, bf16[48,1024]{1,...) custom-call(bf16[4,2,2,2,32,2048]{5,4,3,2,1,0:T(8,128)(2,1)} %bitcast.243, ...), custom_call_target="tpu_custom_call" | custom-call | tf_op jit(solution)/shard_map/reduce_grads/pallas_call | solution.py:455
  281.2 1.2 slice.143
  283.1 2.3 copy.25
  285.4 1.9 copy.47
  287.2 0.8 copy.48
  288.0 0.6 copy.49
  288.7 0.6 copy.50
  (109 shorter events, 10.0 us)
Async XLA Ops:
  0.6 3.3 %copy-start = (s32[4,4,96]{2,1,0:T(4,128)S(1)}, s32[4,4,96]{2,1,0:T(4,128)}, u32[]{:S(2)}) copy-start(s32[4,4,96]{2,1,0:T(4,128)} %param.10) | copy-start | bytes 18436
  0.6 6.6 %copy-start.2 = (bf16[4,1,1,192,1024]{4,3,2,1,0:T(8,128)(2,1)S(1)}, bf16[4,1,1,192,1024]{4,3,2,1,0:T(8,128)(2,1)}, u32[]{:S(2)}) copy-start(bf16[4,1,1,192,1024]{4,3,2,1,0:T(8,128)(2,1)} %param.12) | copy-start | bytes 4718596
  0.7 6.5 %copy-start.20 = (s32[4]{0:T(128)S(1)}, s32[4]{0:T(128)}, u32[]{:S(2)}) copy-start(s32[4]{0:T(128)} %param.11) | copy-start | bytes 52
  10.5 3.1 %copy-start.17 = (bf16[48,2,7,384]{3,1,2,0:T(2,128)(2,1)S(1)}, bf16[48,2,7,384]{3,1,2,0:T(2,128)(2,1)}, u32[]{:S(2)}) copy-start(bf16[48,2,7,384]{3,1,2,0:T(2,128)(2,1)} %param.16) | copy-start | bytes 1548292
  10.9 3.5 %copy-start.3 = (bf16[1,4,96,1024]{3,2,1,0:T(8,128)(2,1)S(1)}, bf16[1,4,96,1024]{3,2,1,0:T(8,128)(2,1)}, u32[]{:S(2)}) copy-start(bf16[1,4,96,1024]{3,2,1,0:T(8,128)(2,1)} %param.9) | copy-start | bytes 2359300
  89.1 6.3 %copy-start.22 = (bf16[4,2,2,2,64,1024]{5,4,3,2,1,0:T(8,128)(2,1)S(1)}, bf16[4,2,2,2,64,1024]{5,4,3,2,1,0:T(8,128)(2,1)}, u32[]{:S(2)}) copy-start(bf16[4,2,2,2,64,1024]{5,4,3,2,1,0:T(8,128)(2,1)} %get-tuple-element.20) | copy-start | bytes 12582916
  95.4 1.8 copy-start.30
  95.4 1.8 copy-start.13
  97.3 1.3 copy-start.27
  99.6 1.9 copy-start.8
  108.1 3.4 %copy-start.9 = (bf16[4,192,2688]{2,1,0:T(8,128)(2,1)S(1)}, bf16[4,192,2688]{2,1,0:T(8,128)(2,1)}, u32[]{:S(2)}) copy-start(bf16[4,192,2688]{2,1,0:T(8,128)(2,1)} %copy-done.8) | copy-start | bytes 12386308
  110.8 3.1 %copy-start.4 = (bf16[1,7,4,2,48,384]{5,4,3,2,1,0:T(8,128)(2,1)}, bf16[1,7,4,2,48,384]{5,4,3,2,1,0:T(8,128)(2,1)S(1)}, u32[]{:S(2)}) copy-start(bf16[1,7,4,2,48,384]{5,4,3,2,1,0:T(8,128)(2,1)S(1)} %get-tuple-element.63) | copy-start | bytes 6193156
  110.8 5.0 %copy-start.6 = (bf16[1,7,4,2,48,384]{5,4,3,2,1,0:T(8,128)(2,1)}, bf16[1,7,4,2,48,384]{5,4,3,2,1,0:T(8,128)(2,1)S(1)}, u32[]{:S(2)}) copy-start(bf16[1,7,4,2,48,384]{5,4,3,2,1,0:T(8,128)(2,1)S(1)} %get-tuple-element.62) | copy-start | bytes 6193156
  115.8 2.4 copy-start.10
  125.1 1.4 copy-start.24
  125.1 1.6 copy-start.25
  126.7 2.9 %copy-start.15 = (bf16[768,384]{1,0:T(8,128)(2,1)}, bf16[768,384]{1,0:T(8,128)(2,1)S(1)}, u32[]{:S(2)}) copy-start(bf16[768,384]{1,0:T(8,128)(2,1)S(1)} %add_convert_fusion) | copy-start | bytes 1769476
  130.9 3.5 %copy-start.26 = (bf16[4,2,48,1024]{3,2,1,0:T(8,128)(2,1)S(1)}, bf16[4,2,48,1024]{3,2,1,0:T(8,128)(2,1)}, u32[]{:S(2)}) copy-start(bf16[4,2,48,1024]{3,2,1,0:T(8,128)(2,1)} %get-tuple-element.23) | copy-start | bytes 2359300
  130.9 3.5 %copy-start.29 = (bf16[768,1024]{1,0:T(8,128)(2,1)S(1)}, bf16[768,1024]{1,0:T(8,128)(2,1)}, u32[]{:S(2)}) copy-start(bf16[768,1024]{1,0:T(8,128)(2,1)} %get-tuple-element.61) | copy-start | bytes 4718596
  134.4 2.2 copy-start.12
  136.5 2.4 copy-start.7
  142.0 2.2 copy-start.11
  146.5 2.4 copy-start.5
  148.9 3.3 %copy-start.28 = (bf16[384,1024]{1,0:T(8,128)(2,1)S(1)}, bf16[384,1024]{1,0:T(8,128)(2,1)}, u32[]{:S(2)}) copy-start(bf16[384,1024]{1,0:T(8,128)(2,1)} %copy-done.27) | copy-start | bytes 2359300
  151.3 3.1 %copy-start.23 = (bf16[4,2,2,2,64,1024]{5,4,3,2,1,0:T(8,128)(2,1)S(1)}, bf16[4,2,2,2,64,1024]{5,4,3,2,1,0:T(8,128)(2,1)}, u32[]{:S(2)}) copy-start(bf16[4,2,2,2,64,1024]{5,4,3,2,1,0:T(8,128)(2,1)} %get-tuple-element.20) | copy-start | bytes 12582916
  152.2 1.6 copy-start.14
  152.2 3.0 %copy-start.32 = (f32[384,2048]{1,0:T(8,128)S(1)}, f32[384,2048]{1,0:T(8,128)}, u32[]{:S(2)}) copy-start(f32[384,2048]{1,0:T(8,128)} %get-tuple-element.67) | copy-start | bytes 9437188
  155.2 3.0 %copy-start.21 = (bf16[4,2,2,2,32,2048]{5,4,3,2,1,0:T(8,128)(2,1)S(1)}, bf16[4,2,2,2,32,2048]{5,4,3,2,1,0:T(8,128)(2,1)}, u32[]{:S(2)}) copy-start(bf16[4,2,2,2,32,2048]{5,4,3,2,1,0:T(8,128)(2,1)} %get-tuple-element.19) | copy-start | bytes 12582916
  160.2 1.5 copy-start.31
  281.2 6.1 %copy-start.16 = (bf16[2,2,64,1024]{3,2,1,0:T(8,128)(2,1)S(1)}, bf16[2,2,64,1024]{3,2,1,0:T(8,128)(2,1)}, u32[]{:S(2)}) copy-start(bf16[2,2,64,1024]{3,2,1,0:T(8,128)(2,1)} %get-tuple-element.27) | copy-start | bytes 1572868
  281.2 6.9 %copy-start.19 = (bf16[2,64,384]{2,1,0:T(8,128)(2,1)S(1)}, bf16[2,64,384]{2,1,0:T(8,128)(2,1)}, u32[]{:S(2)}) copy-start(bf16[2,64,384]{2,1,0:T(8,128)(2,1)} %get-tuple-element.28) | copy-start | bytes 294916
  283.1 6.2 %copy-start.1 = (s32[4,4,96]{2,1,0:T(4,128)S(1)}, s32[4,4,96]{2,1,0:T(4,128)}, u32[]{:S(2)}) copy-start(s32[4,4,96]{2,1,0:T(4,128)} %param.10) | copy-start | bytes 18436
  283.1 5.6 %copy-start.18 = (bf16[48,1024]{1,0:T(8,128)(2,1)S(1)}, bf16[48,1024]{1,0:T(8,128)(2,1)}, u32[]{:S(2)}) copy-start(bf16[48,1024]{1,0:T(8,128)(2,1)} %get-tuple-element.91) | copy-start | bytes 294916
